TPU v7x, 32 devices: a whole 2x2x4 slice. The times are simulated.
32 devices in a mesh: batch: 8 (over z, y), seq: 4 (over x, core).
Axes of the slice: x: 2, y: 2, z: 4, core: 2. Of those that a mesh axis runs over, the one named last changes fastest.
Arguments:
- forward_embed: bfloat16 [12288, 1536], P(('batch', 'seq')), parts along dimension 0, may hold values from -6 to 6
- reverse_embed: bfloat16 [12288, 1536], P(('batch', 'seq')), parts along dimension 0, may hold values from -6 to 6
- conv_weight: bfloat16 [1, 3, 1536, 1536], P(None, None, 'seq'), may hold values from -0.09375 to 0.09375
- conv_bias: float32 [1, 1536], replicated, may hold values from -0.5 to 0.5
- head_weight: bfloat16 [1536, 1024], replicated, may hold values from -0.15625 to 0.15625
- head_bias: float32 [1024], replicated, may hold values from -1 to 1
Outputs:
- averaged: bfloat16 [12288, 1024], P(('batch', 'seq')), parts along dimension 0
There are 8 independent parts, one for each index of `batch`. A program takes and returns all parts, laid end to end along the dimension named above; an argument that names none is the same for every part. Nothing has to cross between parts.
All inputs are finite; a program needn't handle non-finite values.
Results may differ from a plain program's by a relative error of at most 0.008.
Values may be sent and summed in bfloat16 or wider, within the bound.
A program may use at most 128 MiB of HBM per device.

v0:
```python
import functools
import math

import jax
import jax.numpy as jnp
from jax import lax
from jax.experimental import pallas as pl
from jax.experimental.pallas import tpu as pltpu
from jax.sharding import PartitionSpec as P

MESH = pl.DeviceIdType.MESH
F32 = jnp.float32
BF16 = jnp.bfloat16
LANES = 128
WIDE = 256
SPLIT = 2
LAG = 2


def gelu(x):
    return (0.5 * x) * (1.0 + lax.erf(x * math.sqrt(0.5)))


def softplus(x):
    u = jnp.exp(-jnp.abs(x))
    return jnp.maximum(x, 0.0) + jnp.where(u < 1e-3, u - 0.5 * u * u, jnp.log(1.0 + u))


def kernel(
    taps, fwd_hbm, rev_hbm, w_hbm, cb_ref, hw_hbm, hb_ref, fwd_out, rev_out,
    embed, halo, guest, xcat, wbuf, acc, headw, logits, flip, sendt, keept,
    local_sem, halo_send, halo_recv, own_send, own_recv,
    x_send, x_recv, y_send, y_recv, z_send, z_recv, m_send, m_recv, t_send, t_recv, out_sem, guest_sem,
):
    s = lax.axis_index("seq")
    b = lax.axis_index("batch")
    core = s % 2
    far = s // 2
    mate = s + 1 - 2 * core
    across = s + 2 - 4 * far
    mirror = 3 - s
    shards = (s, mate, across, mirror)
    y = b % 2
    z = (b // 2) % 2
    yp = b + 1 - 2 * y
    zp = b + 2 - 4 * z
    cx = y + (1 - y) * 2 * z
    cy = (1 - y) + y * 2 * z
    cz = 2 * (1 - z)
    rows, channels = embed.shape[1:]
    depth = w_hbm.shape[2]
    wide = WIDE
    blocks = channels // wide
    units = SPLIT * blocks
    part = depth // SPLIT
    half = 2 * taps * depth
    tracks = hb_ref.shape[1]
    pieces = tracks // wide
    visit = guest.shape[0] - halo.shape[2]
    kept = rows - visit

    barrier = pltpu.get_barrier_semaphore()
    for peer in ({"seq": mate}, {"seq": across}, {"seq": mirror}, {"batch": yp}, {"batch": zp}):
        pl.semaphore_signal(barrier, inc=1, device_id=peer, device_id_type=MESH)

    loads = [
        pltpu.make_async_copy(fwd_hbm, embed.at[0], local_sem.at[0]),
        pltpu.make_async_copy(rev_hbm, embed.at[1], local_sem.at[1]),
        pltpu.make_async_copy(hw_hbm, headw, local_sem.at[2]),
    ] + [
        pltpu.make_async_copy(
            w_hbm.at[0, k, :, pl.ds(m * wide, wide)], wbuf.at[m, pl.ds(k * depth, depth)], local_sem.at[3 + k * blocks + m]
        )
        for m in range(blocks)
        for k in range(taps)
    ]
    for copy in loads:
        copy.start()
    pl.semaphore_wait(barrier, 5)

    def remote(src, dst, send, recv, peer):
        return pltpu.make_async_remote_copy(
            src_ref=src, dst_ref=dst, send_sem=send, recv_sem=recv, device_id=peer, device_id_type=MESH
        )

    tile = halo.shape[2]
    halos = []
    for k, src in enumerate((fwd_hbm, rev_hbm)):
        halos.append(remote(src.at[pl.ds(rows - tile, tile)], halo.at[k, 0], halo_send.at[k, 0], halo_recv.at[k, 0], {"seq": (s + 1) % 4}))
        target = (s + 3) % 4 if k == 0 else across
        halos.append(remote(src.at[pl.ds(0, tile)], halo.at[k, 1], halo_send.at[k, 1], halo_recv.at[k, 1], {"seq": target}))
    for copy in halos:
        copy.start()

    def cell(slot, tap, unit):
        row = pl.multiple_of((slot * taps + tap) * depth + (unit % SPLIT) * part, 32)
        return wbuf.at[unit // SPLIT, pl.ds(row, part)]

    def x_copy(j):
        row = pl.ds(pl.multiple_of((j % SPLIT) * part, 32), part)
        col = pl.ds(pl.multiple_of((j // SPLIT) * wide, wide), wide)
        return remote(w_hbm.at[0, cx, row, col], cell(2, cx, j), x_send.at[j], x_recv.at[j], {"seq": across})

    def y_copy(color, j):
        return remote(cell(2, color, j), cell(2, color, j), y_send.at[j], y_recv.at[j], {"batch": yp})

    def z_copy(color, j):
        return remote(cell(2, color, j), cell(2, color, j), z_send.at[j], z_recv.at[j], {"batch": zp})

    def m_copy(kind, color, j):
        return remote(cell(2, color, j), cell(3, color, j), m_send.at[kind, j], m_recv.at[kind, j], {"seq": mate})

    guests = remote(
        rev_hbm.at[pl.ds(kept - tile, visit + tile)], guest, guest_sem.at[0], guest_sem.at[1], {"seq": mirror}
    )
    own = [
        remote(
            w_hbm.at[0, k, :, pl.ds(m * wide, wide)], wbuf.at[m, pl.ds((taps + k) * depth, depth)],
            own_send.at[k, m], own_recv.at[k, m], {"seq": mate},
        )
        for m in range(blocks)
        for k in range(taps)
    ]

    def start_x(j, c):
        x_copy(j).start()
        return c

    lax.fori_loop(0, units, start_x, 0)
    for copy in own:
        copy.start()

    r = lax.broadcasted_iota(jnp.int32, (rows, rows), 0)
    c = lax.broadcasted_iota(jnp.int32, (rows, rows), 1)
    flip[...] = jnp.where(r + c == rows - 1, 1.0, 0.0).astype(BF16)
    for k in range(2):
        logits[k] = jnp.broadcast_to(hb_ref[...], (rows, tracks))

    line = lax.broadcasted_iota(jnp.int32, (rows, depth), 0)

    def shard_of(slot):
        return (far + (slot // 2) * (1 - 2 * far)) * 2 + core + (slot % 2) * (1 - 2 * core)

    def build_guest(slot, carry):
        cols = pl.ds(pl.multiple_of(shard_of(slot) * depth, LANES), depth)
        full = guest[:, cols].astype(F32)
        high = jnp.where(s == 2, embed[1, pl.ds(0, tile), cols], halo[1, 1, :, cols]).astype(F32)[0:1]
        high = jnp.where(s == 0, 0.0, high)
        before = pltpu.roll(full, 1, 0)[tile:]
        after = pltpu.roll(full, visit + tile - 1, 0)[tile:]
        after = jnp.where(lax.broadcasted_iota(jnp.int32, (visit, depth), 0) == visit - 1, high, after)
        for tap, value in enumerate((before, full[tile:], after)):
            place = pl.ds(pl.multiple_of((slot * taps + tap) * depth, LANES), depth)
            xcat[1, pl.ds(kept, visit), place] = value.astype(BF16)
        return carry

    def build(k, slot):
        shard = shard_of(slot)
        cols = pl.ds(pl.multiple_of(shard * depth, LANES), depth)
        mid = embed[k, :, cols]
        wide_mid = mid.astype(F32)
        low = halo[k, 0, :, cols].astype(F32)[tile - 1 : tile]
        high = halo[k, 1, :, cols].astype(F32)[0:1]
        low = jnp.where(s == 0, 0.0, low)
        high = jnp.where(s == 3, 0.0, high)
        before = jnp.where(line == 0, low, pltpu.roll(wide_mid, 1, 0))
        after = jnp.where(line == rows - 1, high, pltpu.roll(wide_mid, rows - 1, 0))
        for tap, value in enumerate((before.astype(BF16), mid, after.astype(BF16))):
            xcat[k, :, pl.ds(pl.multiple_of((slot * taps + tap) * depth, LANES), depth)] = value

    def near(k, m):
        cols = pl.ds(pl.multiple_of(m * wide, wide), wide)
        own_rows = pl.ds(0, kept if k else rows)
        acc[k, own_rows, cols] = (
            jnp.dot(xcat[k, own_rows, pl.ds(0, half)], wbuf[m, pl.ds(0, half)], preferred_element_type=F32)
            + cb_ref[:, cols]
        )

    def remote_part(k, m):
        cols = pl.ds(pl.multiple_of(m * wide, wide), wide)
        own_rows = pl.ds(0, kept if k else rows)
        total = acc[k, own_rows, cols] + jnp.dot(
            xcat[k, own_rows, pl.ds(half, half)], wbuf[m, pl.ds(half, half)], preferred_element_type=F32
        )
        hidden = gelu(total).astype(BF16)
        logits[k, own_rows] = logits[k, own_rows] + jnp.dot(hidden, headw[cols, :], preferred_element_type=F32)

    def guest_part(m, carry):
        cols = pl.ds(pl.multiple_of(m * wide, wide), wide)
        part_rows = pl.ds(kept, visit)
        total = jnp.dot(xcat[1, part_rows, :], wbuf[m], preferred_element_type=F32) + cb_ref[:, cols]
        hidden = gelu(total).astype(BF16)
        logits[1, part_rows] = logits[1, part_rows] + jnp.dot(hidden, headw[cols, :], preferred_element_type=F32)
        return carry

    for copy in loads[:2]:
        copy.wait()
    for copy in halos:
        copy.wait()

    def first(i, carry):
        build(i % 2, i // 2)
        return carry

    lax.fori_loop(0, 4, first, 0)

    def step(j, carry):
        @pl.when(j < units)
        def _():
            x_copy(j).wait_recv()
            y_copy(cx, j).start()

            @pl.when(y == 0)
            def _():
                z_copy(cx, j).start()

            m_copy(0, cx, j).start()

        @pl.when((j >= LAG) & (j < units + LAG))
        def _():
            y_copy(cy, j - LAG).wait_recv()

            @pl.when(y == 1)
            def _():
                z_copy(cy, j - LAG).start()

            m_copy(1, cy, j - LAG).start()

        @pl.when((j >= 2 * LAG) & (j < units + 2 * LAG))
        def _():
            z_copy(cz, j - 2 * LAG).wait_recv()
            m_copy(2, cz, j - 2 * LAG).start()

        @pl.when(j == units - 2)
        def _():
            guests.start()

        @pl.when(j == 0)
        def _():
            lax.fori_loop(4, 8, first, 0)
            for copy in loads[2:]:
                copy.wait()
            for copy in own:
                copy.wait()

        pace = SPLIT // 2

        @pl.when((j >= 1) & ((j - 1) % pace == 0) & (j < units + 1))
        def _():
            i = (j - 1) // pace

            @pl.when(i % 2 == 0)
            def _():
                near(1, i // 2)

            @pl.when(i % 2 == 1)
            def _():
                near(0, i // 2)

        late = j - SPLIT - 2 * LAG

        @pl.when((late >= 0) & (late % pace == 0))
        def _():
            k = 1 - late // pace % 2
            m = late // SPLIT

            @pl.when(k == 1)
            def _():
                for kind, color in enumerate((cx, cy, cz)):
                    for u in range(SPLIT):
                        m_copy(kind, color, SPLIT * m + u).wait_recv()

                remote_part(1, m)

            @pl.when(k == 0)
            def _():
                remote_part(0, m)

        return carry

    lax.fori_loop(0, units + 2 * LAG + 1, step, 0)

    def t_copy(p):
        cols = pl.ds(p * wide, wide)
        return remote(sendt.at[pl.ds(0, kept), cols], rev_out.at[pl.ds(visit, kept), cols], t_send.at[p], t_recv.at[p], {"seq": mirror})

    for p in range(pieces):
        cols = pl.ds(p * wide, wide)
        value = softplus(logits[1, pl.ds(0, kept), cols]).astype(BF16)
        turn = flip[pl.ds(visit, kept), pl.ds(0, kept)]
        sendt[pl.ds(0, kept), cols] = jnp.dot(turn, value, preferred_element_type=F32).astype(BF16)
        if p:
            t_copy(p - 1).start()
    remote_part(0, blocks - 1)
    t_copy(pieces - 1).start()
    keep = []
    for p in range(pieces):
        cols = pl.ds(p * wide, wide)
        keept[:, cols] = softplus(logits[0, :, cols]).astype(BF16)
        keep.append(pltpu.make_async_copy(keept.at[:, cols], fwd_out.at[:, cols], out_sem.at[p]))
        if p:
            keep[p - 1].start()

    guests.wait_recv()
    keep[-1].start()
    lax.fori_loop(0, 4, build_guest, 0)
    lax.fori_loop(0, blocks, guest_part, 0)
    value = softplus(logits[1, pl.ds(kept, visit)]).astype(BF16)
    turn = flip[pl.ds(0, visit), pl.ds(kept, visit)]
    sendt[pl.ds(kept, visit)] = jnp.dot(turn, value, preferred_element_type=F32).astype(BF16)
    keep.append(pltpu.make_async_copy(sendt.at[pl.ds(kept, visit)], rev_out.at[pl.ds(0, visit)], out_sem.at[pieces]))

    def drain(j, carry):
        x_copy(j).wait_send()
        y_copy(cx, j).wait_send()
        z_copy(2 * z, j).wait_send()
        for kind, color in enumerate((cx, cy, cz)):
            m_copy(kind, color, j).wait_send()
        return carry

    lax.fori_loop(0, units, drain, 0)
    keep[-1].start()
    for copy in keep:
        copy.wait()
    guests.wait_send()
    for p in range(pieces):
        t_copy(p).wait()


def fused(forward_embed, reverse_embed, conv_weight, conv_bias, head_weight, head_bias):
    rows, channels = forward_embed.shape
    _, taps, depth, _ = conv_weight.shape
    tracks = head_weight.shape[1]
    blocks = channels // WIDE
    units = SPLIT * blocks
    pieces = tracks // WIDE
    dma = pltpu.SemaphoreType.DMA
    anywhere = pl.BlockSpec(memory_space=pl.ANY)
    vmem = pl.BlockSpec(memory_space=pltpu.VMEM)
    forward_tracks, reverse_tracks = pl.pallas_call(
        functools.partial(kernel, taps),
        out_shape=[jax.ShapeDtypeStruct((rows, tracks), BF16)] * 2,
        in_specs=[anywhere, anywhere, anywhere, vmem, anywhere, vmem],
        out_specs=[anywhere, anywhere],
        scratch_shapes=[
            pltpu.VMEM((2, rows, channels), BF16),
            pltpu.VMEM((2, 2, 16, channels), BF16),
            pltpu.VMEM((rows // 2 + 16, channels), BF16),
            pltpu.VMEM((2, rows, 4 * taps * depth), BF16),
            pltpu.VMEM((blocks, 4 * taps * depth, WIDE), BF16),
            pltpu.VMEM((2, rows, channels), F32),
            pltpu.VMEM((channels, tracks), BF16),
            pltpu.VMEM((2, rows, tracks), F32),
            pltpu.VMEM((rows, rows), BF16),
            pltpu.VMEM((rows, tracks), BF16),
            pltpu.VMEM((rows, tracks), BF16),
            dma((3 + taps * blocks,)),
            dma((2, 2)), dma((2, 2)),
            dma((taps, blocks)), dma((taps, blocks)),
            dma((units,)), dma((units,)),
            dma((units,)), dma((units,)),
            dma((units,)), dma((units,)),
            dma((3, units)), dma((3, units)),
            dma((pieces,)), dma((pieces,)), dma((pieces + 1,)), dma((2,)),
        ],
        compiler_params=pltpu.CompilerParams(
            collective_id=0, has_side_effects=True, vmem_limit_bytes=62 * 1024 * 1024
        ),
    )(forward_embed, reverse_embed, conv_weight, conv_bias, head_weight, head_bias[None])
    return (0.5 * (forward_tracks.astype(F32) + reverse_tracks.astype(F32))).astype(BF16)


def with_halo(block, axis):
    count = lax.axis_size(axis)
    forward = [(i, i + 1) for i in range(count - 1)]
    backward = [(target, source) for source, target in forward]
    low = lax.ppermute(block[-1:], axis, forward)
    high = lax.ppermute(block[:1], axis, backward)
    return jnp.concatenate([low, block, high], axis=0)


def general(forward_embed, reverse_embed, conv_weight, conv_bias, head_weight, head_bias):
    count = lax.axis_size("seq")
    layers, taps = conv_weight.shape[:2]
    gathered = [lax.all_gather(conv_weight[n], "seq", axis=1, tiled=True) for n in range(layers)]

    def strand(hidden):
        for n in range(layers):
            rows = hidden.shape[0]
            padded = with_halo(hidden, "seq")
            total = sum(
                jnp.dot(padded[k : k + rows], gathered[n][k], preferred_element_type=F32) for k in range(taps)
            )
            hidden = jax.nn.gelu(total + conv_bias[n], approximate=False).astype(BF16)
        logits = jnp.dot(hidden, head_weight, preferred_element_type=F32) + head_bias
        return jax.nn.softplus(logits).astype(BF16)

    reverse_tracks = strand(reverse_embed)[::-1]
    reverse_tracks = lax.ppermute(reverse_tracks, "seq", [(i, count - 1 - i) for i in range(count)])
    mean = 0.5 * (strand(forward_embed).astype(F32) + reverse_tracks.astype(F32))
    return mean.astype(BF16)


def solution(mesh):
    cubes = mesh.shape["seq"] == 4 and mesh.shape["batch"] % 4 == 0
    return jax.shard_map(
        fused if cubes else general,
        mesh=mesh,
        in_specs=(
            P(("batch", "seq"), None),
            P(("batch", "seq"), None),
            P(None, None, "seq", None),
            P(),
            P(),
            P(),
        ),
        out_specs=P(("batch", "seq"), None),
        check_vma=False,
    )
```

profile of v0, /device:TPU:1, one launch (start us, length us, event | category | flops | bytes accessed | tf_op | source)
XLA Modules:
  0.0 60.6 jit_solution(13755412726411419494)
XLA Ops:
  0.0 58.1 %shard_map.64 = (bf16[384,1024]{1,0:T(8,128)(2,1)}, bf16[384,1024]{1,0:T(8,128)(2,1)}) custom-call(bf16[384,1536]{1,0:T(8,128)(2,1)} %fwd_hbm.1, bf16[384,1536]{1,0:T(8,128)(2,1)} %rev_hbm.1, bf16[1,3,384,1536]{3,2,1,0:T(8,128)(2,1)} %w_hbm.1, f32[1,1536]{1,0:T(1,128)} %cb_ref.1, bf16[1536,1024]{1,0:T(8,128)(2,1)} %hw_hbm.1, f32[1,1024]{1,0:T(1,128)} %bitcast.1), custom_call_target="tpu_custom_call" | custom-call | tf_op jit(solution)/shard_map/pallas_call | solution.py:340
  58.1 2.5 %multiply_convert_fusion = bf16[384,1024]{1,0:T(8,128)(2,1)} fusion(bf16[384,1024]{1,0:T(8,128)(2,1)} %get-tuple-element.8, bf16[384,1024]{1,0:T(8,128)(2,1)} %get-tuple-element.7), kind=kLoop, calls=%fused_computation | loop fusion | flops 1966080 | bytes 2359296 | tf_op jit(solution)/shard_map/convert_element_type | solution.py:370
where the time goes:
time: 60.8 us; the launch traced here: 60.6 us
  Pallas kernels  58.1 us (96%)
  other arithmetic  2.53 us (4%)
    pallas_call x1, Pallas kernels, fused(): pl.pallas_call(functools.partial(kernel, taps), out_shape=[jax.ShapeDtype...  58.1 us
    convert_element_type x1, other arithmetic, fused(): (0.5 * (forward_tracks.astype(F32) + reverse_tracks.astype(F32))).astype(...  2.53 us

commit v1 on v0

--- a/solution.py
+++ b/solution.py
@@ -14,7 +14,11 @@
 LANES = 128
 WIDE = 256
 SPLIT = 2
+START = 2
 LAG = 2
+LAG2 = 2
+COLORS = 4
+VISIT = 12
 
 
 def gelu(x):
@@ -27,8 +31,8 @@
 
 
 def kernel(
-    taps, fwd_hbm, rev_hbm, w_hbm, cb_ref, hw_hbm, hb_ref, fwd_out, rev_out,
-    embed, halo, guest, xcat, wbuf, acc, headw, logits, flip, sendt, keept,
+    taps, fwd_hbm, rev_hbm, w_hbm, cb_hbm, hw_hbm, hb_hbm, fwd_out, rev_out,
+    embed, halo, guest, xcat, wbuf, acc, headw, logits, flip, sendt, keept, cb_ref, hb_ref,
     local_sem, halo_send, halo_recv, own_send, own_recv,
     x_send, x_recv, y_send, y_recv, z_send, z_recv, m_send, m_recv, t_send, t_recv, out_sem, guest_sem,
 ):
@@ -44,15 +48,19 @@
     z = (b // 2) % 2
     yp = b + 1 - 2 * y
     zp = b + 2 - 4 * z
-    cx = y + (1 - y) * 2 * z
-    cy = (1 - y) + y * 2 * z
-    cz = 2 * (1 - z)
+    cx = 2 * z + y
+    cy = 2 * z + 1 - y
+    cz = 2 * (1 - z) + y
+    cd = 2 * (1 - z) + 1 - y
     rows, channels = embed.shape[1:]
-    depth = w_hbm.shape[2]
+    deep = w_hbm.shape[0]
+    depth = deep // taps
     wide = WIDE
     blocks = channels // wide
     units = SPLIT * blocks
-    part = depth // SPLIT
+    part = deep // SPLIT
+    grain = part // COLORS
+    thin = wide // 2
     half = 2 * taps * depth
     tracks = hb_ref.shape[1]
     pieces = tracks // wide
@@ -63,18 +71,20 @@
     for peer in ({"seq": mate}, {"seq": across}, {"seq": mirror}, {"batch": yp}, {"batch": zp}):
         pl.semaphore_signal(barrier, inc=1, device_id=peer, device_id_type=MESH)
 
+    small = [
+        pltpu.make_async_copy(cb_hbm, cb_ref, local_sem.at[4]),
+        pltpu.make_async_copy(hb_hbm, hb_ref, local_sem.at[5]),
+    ]
     loads = [
         pltpu.make_async_copy(fwd_hbm, embed.at[0], local_sem.at[0]),
         pltpu.make_async_copy(rev_hbm, embed.at[1], local_sem.at[1]),
         pltpu.make_async_copy(hw_hbm, headw, local_sem.at[2]),
-    ] + [
-        pltpu.make_async_copy(
-            w_hbm.at[0, k, :, pl.ds(m * wide, wide)], wbuf.at[m, pl.ds(k * depth, depth)], local_sem.at[3 + k * blocks + m]
-        )
+    ]
+    chunks = [
+        pltpu.make_async_copy(w_hbm.at[:, pl.ds(m * wide, wide)], wbuf.at[m, pl.ds(0, deep)], local_sem.at[3])
         for m in range(blocks)
-        for k in range(taps)
     ]
-    for copy in loads:
+    for copy in small + loads[:2] + chunks + loads[2:]:
         copy.start()
     pl.semaphore_wait(barrier, 5)
 
@@ -84,55 +94,71 @@
         )
 
     tile = halo.shape[2]
-    halos = []
-    for k, src in enumerate((fwd_hbm, rev_hbm)):
-        halos.append(remote(src.at[pl.ds(rows - tile, tile)], halo.at[k, 0], halo_send.at[k, 0], halo_recv.at[k, 0], {"seq": (s + 1) % 4}))
-        target = (s + 3) % 4 if k == 0 else across
-        halos.append(remote(src.at[pl.ds(0, tile)], halo.at[k, 1], halo_send.at[k, 1], halo_recv.at[k, 1], {"seq": target}))
-    for copy in halos:
-        copy.start()
-
-    def cell(slot, tap, unit):
-        row = pl.multiple_of((slot * taps + tap) * depth + (unit % SPLIT) * part, 32)
-        return wbuf.at[unit // SPLIT, pl.ds(row, part)]
+
+    def halo_copy(k, side, target):
+        src = (fwd_hbm, rev_hbm)[k].at[pl.ds(0 if side else rows - tile, tile)]
+        return remote(src, halo.at[k, side], halo_send.at[k, side], halo_recv.at[k, side], {"seq": target})
+
+    def cell(slot, color, j):
+        row = pl.multiple_of(slot * deep + (j % SPLIT) * part + color * grain, tile)
+        return wbuf.at[j // SPLIT, pl.ds(row, grain)]
 
     def x_copy(j):
-        row = pl.ds(pl.multiple_of((j % SPLIT) * part, 32), part)
+        row = pl.ds(pl.multiple_of((j % SPLIT) * part + cx * grain, tile), grain)
         col = pl.ds(pl.multiple_of((j // SPLIT) * wide, wide), wide)
-        return remote(w_hbm.at[0, cx, row, col], cell(2, cx, j), x_send.at[j], x_recv.at[j], {"seq": across})
-
-    def y_copy(color, j):
-        return remote(cell(2, color, j), cell(2, color, j), y_send.at[j], y_recv.at[j], {"batch": yp})
-
-    def z_copy(color, j):
-        return remote(cell(2, color, j), cell(2, color, j), z_send.at[j], z_recv.at[j], {"batch": zp})
-
-    def m_copy(kind, color, j):
-        return remote(cell(2, color, j), cell(3, color, j), m_send.at[kind, j], m_recv.at[kind, j], {"seq": mate})
+        return remote(w_hbm.at[row, col], cell(2, cx, j), x_send, x_recv.at[j], {"seq": across})
+
+    def y_copy(kind, j):
+        ref = cell(2, cz, j).at[:, pl.ds(thin, thin)] if kind else cell(2, cx, j)
+        return remote(ref, ref, y_send.at[kind], y_recv.at[kind, j], {"batch": yp})
+
+    def z_copy(kind, j):
+        ref = cell(2, cy, j).at[:, pl.ds(0, thin)] if kind else cell(2, cx, j)
+        return remote(ref, ref, z_send.at[kind], z_recv.at[kind, j], {"batch": zp})
+
+    def m_copy(color, j):
+        return remote(cell(2, color, j), cell(3, color, j), m_send, m_recv.at[j // SPLIT], {"seq": mate})
+
+    def stripe(share):
+        return wbuf.at[:, pl.ds(0, deep // share)]
 
     guests = remote(
         rev_hbm.at[pl.ds(kept - tile, visit + tile)], guest, guest_sem.at[0], guest_sem.at[1], {"seq": mirror}
     )
     own = [
-        remote(
-            w_hbm.at[0, k, :, pl.ds(m * wide, wide)], wbuf.at[m, pl.ds((taps + k) * depth, depth)],
-            own_send.at[k, m], own_recv.at[k, m], {"seq": mate},
-        )
+        remote(w_hbm.at[:, pl.ds(m * wide, wide)], wbuf.at[m, pl.ds(deep, deep)], own_send, own_recv, {"seq": mate})
         for m in range(blocks)
-        for k in range(taps)
     ]
 
     def start_x(j, c):
         x_copy(j).start()
         return c
 
-    lax.fori_loop(0, units, start_x, 0)
+    lax.fori_loop(0, SPLIT, start_x, 0)
+
+    @pl.when(s < 3)
+    def _():
+        halo_copy(0, 0, s + 1).start()
+        halo_copy(1, 0, s + 1).start()
+
+    @pl.when(s > 0)
+    def _():
+        halo_copy(0, 1, s - 1).start()
+
+    @pl.when(core == 1)
+    def _():
+        halo_copy(1, 1, across).start()
+
+    lax.fori_loop(SPLIT, units, start_x, 0)
+    guests.start()
     for copy in own:
         copy.start()
 
     r = lax.broadcasted_iota(jnp.int32, (rows, rows), 0)
     c = lax.broadcasted_iota(jnp.int32, (rows, rows), 1)
     flip[...] = jnp.where(r + c == rows - 1, 1.0, 0.0).astype(BF16)
+    for copy in small:
+        copy.wait()
     for k in range(2):
         logits[k] = jnp.broadcast_to(hb_ref[...], (rows, tracks))
 
@@ -144,8 +170,7 @@
     def build_guest(slot, carry):
         cols = pl.ds(pl.multiple_of(shard_of(slot) * depth, LANES), depth)
         full = guest[:, cols].astype(F32)
-        high = jnp.where(s == 2, embed[1, pl.ds(0, tile), cols], halo[1, 1, :, cols]).astype(F32)[0:1]
-        high = jnp.where(s == 0, 0.0, high)
+        high = halo[1, 1, :, cols].astype(F32)[0:1]
         before = pltpu.roll(full, 1, 0)[tile:]
         after = pltpu.roll(full, visit + tile - 1, 0)[tile:]
         after = jnp.where(lax.broadcasted_iota(jnp.int32, (visit, depth), 0) == visit - 1, high, after)
@@ -161,8 +186,6 @@
         wide_mid = mid.astype(F32)
         low = halo[k, 0, :, cols].astype(F32)[tile - 1 : tile]
         high = halo[k, 1, :, cols].astype(F32)[0:1]
-        low = jnp.where(s == 0, 0.0, low)
-        high = jnp.where(s == 3, 0.0, high)
         before = jnp.where(line == 0, low, pltpu.roll(wide_mid, 1, 0))
         after = jnp.where(line == rows - 1, high, pltpu.roll(wide_mid, rows - 1, 0))
         for tap, value in enumerate((before.astype(BF16), mid, after.astype(BF16))):
@@ -193,61 +216,76 @@
         logits[1, part_rows] = logits[1, part_rows] + jnp.dot(hidden, headw[cols, :], preferred_element_type=F32)
         return carry
 
-    for copy in loads[:2]:
-        copy.wait()
-    for copy in halos:
-        copy.wait()
-
     def first(i, carry):
         build(i % 2, i // 2)
         return carry
 
-    lax.fori_loop(0, 4, first, 0)
-
     def step(j, carry):
         @pl.when(j < units)
         def _():
             x_copy(j).wait_recv()
-            y_copy(cx, j).start()
-
-            @pl.when(y == 0)
-            def _():
-                z_copy(cx, j).start()
-
-            m_copy(0, cx, j).start()
+            y_copy(0, j).start()
+            z_copy(0, j).start()
+            m_copy(cx, j).start()
 
         @pl.when((j >= LAG) & (j < units + LAG))
         def _():
-            y_copy(cy, j - LAG).wait_recv()
-
-            @pl.when(y == 1)
-            def _():
-                z_copy(cy, j - LAG).start()
-
-            m_copy(1, cy, j - LAG).start()
-
-        @pl.when((j >= 2 * LAG) & (j < units + 2 * LAG))
-        def _():
-            z_copy(cz, j - 2 * LAG).wait_recv()
-            m_copy(2, cz, j - 2 * LAG).start()
-
-        @pl.when(j == units - 2)
-        def _():
-            guests.start()
-
-        @pl.when(j == 0)
-        def _():
-            lax.fori_loop(4, 8, first, 0)
-            for copy in loads[2:]:
+            y_copy(0, j - LAG).wait_recv()
+            z_copy(1, j - LAG).start()
+            m_copy(cy, j - LAG).start()
+            z_copy(0, j - LAG).wait_recv()
+            y_copy(1, j - LAG).start()
+            m_copy(cz, j - LAG).start()
+
+        @pl.when((j >= LAG + LAG2) & (j < units + LAG + LAG2))
+        def _():
+            y_copy(1, j - LAG - LAG2).wait_recv()
+            z_copy(1, j - LAG - LAG2).wait_recv()
+            m_copy(cd, j - LAG - LAG2).start()
+
+        @pl.when(j == START)
+        def _():
+            for copy in loads[:2]:
                 copy.wait()
-            for copy in own:
-                copy.wait()
+
+            @pl.when(s == 0)
+            def _():
+                halo[0, 0] = jnp.zeros_like(halo[0, 0])
+                halo[1, 0] = jnp.zeros_like(halo[1, 0])
+                halo[1, 1] = jnp.zeros_like(halo[1, 1])
+
+            @pl.when(s == 3)
+            def _():
+                halo[0, 1] = jnp.zeros_like(halo[0, 1])
+
+            @pl.when(s == 2)
+            def _():
+                halo[1, 1] = embed[1, pl.ds(0, tile)]
+
+            @pl.when(s > 0)
+            def _():
+                halo_copy(0, 0, mate).wait_recv()
+                halo_copy(1, 0, mate).wait_recv()
+
+            @pl.when(s < 3)
+            def _():
+                halo_copy(0, 1, mate).wait_recv()
+
+            @pl.when(core == 1)
+            def _():
+                halo_copy(1, 1, across).wait_recv()
+
+            lax.fori_loop(0, 8, first, 0)
+            loads[2].wait()
+            whole = wbuf.at[:, pl.ds(0, deep)]
+            pltpu.make_async_copy(whole, whole, local_sem.at[3]).wait()
+            remote(whole, wbuf.at[:, pl.ds(deep, deep)], own_send, own_recv, {"seq": mate}).wait()
 
         pace = SPLIT // 2
 
-        @pl.when((j >= 1) & ((j - 1) % pace == 0) & (j < units + 1))
-        def _():
-            i = (j - 1) // pace
+        @pl.when((j > START) & ((j - 1 - START) % pace == 0) & (j < units + 1 + START))
+        def _():
+            i = (j - 1 - START) // pace
 
             @pl.when(i % 2 == 0)
             def _():
@@ -257,7 +295,7 @@
             def _():
                 near(0, i // 2)
 
-        late = j - SPLIT - 2 * LAG
+        late = j - SPLIT - LAG - LAG2
 
         @pl.when((late >= 0) & (late % pace == 0))
         def _():
@@ -266,10 +304,8 @@
 
             @pl.when(k == 1)
             def _():
-                for kind, color in enumerate((cx, cy, cz)):
-                    for u in range(SPLIT):
-                        m_copy(kind, color, SPLIT * m + u).wait_recv()
-
+                full = wbuf.at[m, pl.ds(0, deep)]
+                remote(full, full, m_send, m_recv.at[m], {"seq": mate}).wait_recv()
                 remote_part(1, m)
 
             @pl.when(k == 0)
@@ -278,7 +314,7 @@
 
         return carry
 
-    lax.fori_loop(0, units + 2 * LAG + 1, step, 0)
+    lax.fori_loop(0, units + LAG + LAG2 + 1, step, 0)
 
     def t_copy(p):
         cols = pl.ds(p * wide, wide)
@@ -310,15 +346,25 @@
     sendt[pl.ds(kept, visit)] = jnp.dot(turn, value, preferred_element_type=F32).astype(BF16)
     keep.append(pltpu.make_async_copy(sendt.at[pl.ds(kept, visit)], rev_out.at[pl.ds(0, visit)], out_sem.at[pieces]))
 
-    def drain(j, carry):
-        x_copy(j).wait_send()
-        y_copy(cx, j).wait_send()
-        z_copy(2 * z, j).wait_send()
-        for kind, color in enumerate((cx, cy, cz)):
-            m_copy(kind, color, j).wait_send()
-        return carry
-
-    lax.fori_loop(0, units, drain, 0)
+    remote(stripe(4), stripe(4), x_send, x_recv.at[0], {"seq": across}).wait_send()
+    for kind, share in ((0, 4), (1, 8)):
+        remote(stripe(share), stripe(share), y_send.at[kind], y_recv.at[kind, 0], {"batch": yp}).wait_send()
+        remote(stripe(share), stripe(share), z_send.at[kind], z_recv.at[kind, 0], {"batch": zp}).wait_send()
+    remote(stripe(1), stripe(1), m_send, m_recv.at[0], {"seq": mate}).wait_send()
+
+    @pl.when(s < 3)
+    def _():
+        halo_copy(0, 0, s + 1).wait_send()
+        halo_copy(1, 0, s + 1).wait_send()
+
+    @pl.when(s > 0)
+    def _():
+        halo_copy(0, 1, s - 1).wait_send()
+
+    @pl.when(core == 1)
+    def _():
+        halo_copy(1, 1, across).wait_send()
+
     keep[-1].start()
     for copy in keep:
         copy.wait()
@@ -336,16 +382,15 @@
     pieces = tracks // WIDE
     dma = pltpu.SemaphoreType.DMA
     anywhere = pl.BlockSpec(memory_space=pl.ANY)
-    vmem = pl.BlockSpec(memory_space=pltpu.VMEM)
     forward_tracks, reverse_tracks = pl.pallas_call(
         functools.partial(kernel, taps),
         out_shape=[jax.ShapeDtypeStruct((rows, tracks), BF16)] * 2,
-        in_specs=[anywhere, anywhere, anywhere, vmem, anywhere, vmem],
+        in_specs=[anywhere] * 6,
         out_specs=[anywhere, anywhere],
         scratch_shapes=[
             pltpu.VMEM((2, rows, channels), BF16),
             pltpu.VMEM((2, 2, 16, channels), BF16),
-            pltpu.VMEM((rows // 2 + 16, channels), BF16),
+            pltpu.VMEM((rows * VISIT // 24 + 16, channels), BF16),
             pltpu.VMEM((2, rows, 4 * taps * depth), BF16),
             pltpu.VMEM((blocks, 4 * taps * depth, WIDE), BF16),
             pltpu.VMEM((2, rows, channels), F32),
@@ -354,19 +399,21 @@
             pltpu.VMEM((rows, rows), BF16),
             pltpu.VMEM((rows, tracks), BF16),
             pltpu.VMEM((rows, tracks), BF16),
-            dma((3 + taps * blocks,)),
+            pltpu.VMEM((1, channels), F32),
+            pltpu.VMEM((1, tracks), F32),
+            dma((6,)),
             dma((2, 2)), dma((2, 2)),
-            dma((taps, blocks)), dma((taps, blocks)),
-            dma((units,)), dma((units,)),
-            dma((units,)), dma((units,)),
-            dma((units,)), dma((units,)),
-            dma((3, units)), dma((3, units)),
+            dma, dma,
+            dma, dma((units,)),
+            dma((2,)), dma((2, units)),
+            dma((2,)), dma((2, units)),
+            dma, dma((blocks,)),
             dma((pieces,)), dma((pieces,)), dma((pieces + 1,)), dma((2,)),
         ],
         compiler_params=pltpu.CompilerParams(
             collective_id=0, has_side_effects=True, vmem_limit_bytes=62 * 1024 * 1024
         ),
-    )(forward_embed, reverse_embed, conv_weight, conv_bias, head_weight, head_bias[None])
+    )(forward_embed, reverse_embed, conv_weight.reshape(taps * depth, channels), conv_bias, head_weight, head_bias[None])
     return (0.5 * (forward_tracks.astype(F32) + reverse_tracks.astype(F32))).astype(BF16)
 
 

time: 60.8 us -> 57.9 us (0.952)
  Pallas kernels: 58.1 us -> 54.6 us
    pallas_call x1, Pallas kernels: 58.1 us -> 54.6 us  [fused(): pl.pallas_call(functools.partial(kernel, taps), out_shape=[jax.ShapeDtype...]
where the time goes in v1:
time: 57.9 us; the launch traced here: 57.1 us
  Pallas kernels  54.6 us (94%)
  other arithmetic  2.53 us (4%)
    pallas_call x1, Pallas kernels, fused(): pl.pallas_call(functools.partial(kernel, taps), out_shape=[jax.ShapeDtype...  54.6 us
    convert_element_type x1, other arithmetic, fused(): (0.5 * (forward_tracks.astype(F32) + reverse_tracks.astype(F32))).astype(...  2.53 us

profile of v1, /device:TPU:1, one launch (start us, length us, event | category | flops | bytes accessed | tf_op | source)
XLA Modules:
  0.0 57.1 jit_solution(17072214864540128532)
XLA Ops:
  0.0 54.6 %shard_map.64 = (bf16[384,1024]{1,0:T(8,128)(2,1)}, bf16[384,1024]{1,0:T(8,128)(2,1)}) custom-call(bf16[384,1536]{1,0:T(8,128)(2,1)} %fwd_hbm.1, bf16[384,1536]{1,0:T(8,128)(2,1)} %rev_hbm.1, bf16[1152,1536]{1,0:T(8,128)(2,1)} %bitcast.2, f32[1,1536]{1,0:T(1,128)} %cb_hbm.1, bf16[1536,1024]{1,0:T(8,128)(2,1)} %hw_hbm.1, f32[1,1024]{1,0:T(1,128)} %bitcast.3), custom_call_target="tpu_custom_call" | custom-call | tf_op jit(solution)/shard_map/pallas_call | solution.py:385
  54.6 2.5 %multiply_convert_fusion = bf16[384,1024]{1,0:T(8,128)(2,1)} fusion(bf16[384,1024]{1,0:T(8,128)(2,1)} %get-tuple-element.8, bf16[384,1024]{1,0:T(8,128)(2,1)} %get-tuple-element.7), kind=kLoop, calls=%fused_computation | loop fusion | flops 1966080 | bytes 2359296 | tf_op jit(solution)/shard_map/convert_element_type | solution.py:417

commit v2 on v1

--- a/solution.py
+++ b/solution.py
@@ -14,11 +14,13 @@
 LANES = 128
 WIDE = 256
 SPLIT = 2
+PAIR = 2
+TILE = 8
 START = 2
 LAG = 2
 LAG2 = 2
 COLORS = 4
-VISIT = 12
+VISIT = 13
 
 
 def gelu(x):
@@ -100,11 +102,11 @@
         return remote(src, halo.at[k, side], halo_send.at[k, side], halo_recv.at[k, side], {"seq": target})
 
     def cell(slot, color, j):
-        row = pl.multiple_of(slot * deep + (j % SPLIT) * part + color * grain, tile)
+        row = pl.multiple_of(slot * deep + (j % SPLIT) * part + color * grain, 16)
         return wbuf.at[j // SPLIT, pl.ds(row, grain)]
 
     def x_copy(j):
-        row = pl.ds(pl.multiple_of((j % SPLIT) * part + cx * grain, tile), grain)
+        row = pl.ds(pl.multiple_of((j % SPLIT) * part + cx * grain, 16), grain)
         col = pl.ds(pl.multiple_of((j // SPLIT) * wide, wide), wide)
         return remote(w_hbm.at[row, col], cell(2, cx, j), x_send, x_recv.at[j], {"seq": across})
 
@@ -208,12 +210,17 @@
         hidden = gelu(total).astype(BF16)
         logits[k, own_rows] = logits[k, own_rows] + jnp.dot(hidden, headw[cols, :], preferred_element_type=F32)
 
-    def guest_part(m, carry):
-        cols = pl.ds(pl.multiple_of(m * wide, wide), wide)
+    def guest_part(i, carry):
         part_rows = pl.ds(kept, visit)
-        total = jnp.dot(xcat[1, part_rows, :], wbuf[m], preferred_element_type=F32) + cb_ref[:, cols]
-        hidden = gelu(total).astype(BF16)
-        logits[1, part_rows] = logits[1, part_rows] + jnp.dot(hidden, headw[cols, :], preferred_element_type=F32)
+        hidden = []
+        for m in (PAIR * i + n for n in range(PAIR)):
+            cols = pl.ds(pl.multiple_of(m * wide, wide), wide)
+            total = jnp.dot(xcat[1, part_rows, :], wbuf[m], preferred_element_type=F32) + cb_ref[:, cols]
+            hidden.append(gelu(total).astype(BF16))
+        span = pl.ds(pl.multiple_of(i * PAIR * wide, wide), PAIR * wide)
+        logits[1, part_rows] = logits[1, part_rows] + jnp.dot(
+            jnp.concatenate(hidden, axis=1), headw[span, :], preferred_element_type=F32
+        )
         return carry
 
     def first(i, carry):
@@ -340,7 +347,7 @@
     guests.wait_recv()
     keep[-1].start()
     lax.fori_loop(0, 4, build_guest, 0)
-    lax.fori_loop(0, blocks, guest_part, 0)
+    lax.fori_loop(0, blocks // PAIR, guest_part, 0)
     value = softplus(logits[1, pl.ds(kept, visit)]).astype(BF16)
     turn = flip[pl.ds(0, visit), pl.ds(kept, visit)]
     sendt[pl.ds(kept, visit)] = jnp.dot(turn, value, preferred_element_type=F32).astype(BF16)
@@ -389,8 +396,8 @@
         out_specs=[anywhere, anywhere],
         scratch_shapes=[
             pltpu.VMEM((2, rows, channels), BF16),
-            pltpu.VMEM((2, 2, 16, channels), BF16),
-            pltpu.VMEM((rows * VISIT // 24 + 16, channels), BF16),
+            pltpu.VMEM((2, 2, TILE, channels), BF16),
+            pltpu.VMEM((rows * VISIT // 24 + TILE, channels), BF16),
             pltpu.VMEM((2, rows, 4 * taps * depth), BF16),
             pltpu.VMEM((blocks, 4 * taps * depth, WIDE), BF16),
             pltpu.VMEM((2, rows, channels), F32),

time: 57.9 us -> 55.7 us (0.962); the launches traced: 57.1 us -> 55.5 us
  Pallas kernels: 54.6 us -> 53 us
    pallas_call x1, Pallas kernels: 54.6 us -> 53 us  [fused(): pl.pallas_call(functools.partial(kernel, taps), out_shape=[jax.ShapeDtype...]
where the time goes in v2:
time: 55.7 us; the launch traced here: 55.5 us
  Pallas kernels  53 us (95%)
  other arithmetic  2.53 us (5%)
    pallas_call x1, Pallas kernels, fused(): pl.pallas_call(functools.partial(kernel, taps), out_shape=[jax.ShapeDtype...  53 us
    convert_element_type x1, other arithmetic, fused(): (0.5 * (forward_tracks.astype(F32) + reverse_tracks.astype(F32))).astype(...  2.53 us

profile of v2, /device:TPU:1, one launch (start us, length us, event | category | flops | bytes accessed | tf_op | source)
XLA Modules:
  0.0 55.5 jit_solution(1912846387180454125)
XLA Ops:
  0.0 53.0 %shard_map.64 = (bf16[384,1024]{1,0:T(8,128)(2,1)}, bf16[384,1024]{1,0:T(8,128)(2,1)}) custom-call(bf16[384,1536]{1,0:T(8,128)(2,1)} %fwd_hbm.1, bf16[384,1536]{1,0:T(8,128)(2,1)} %rev_hbm.1, bf16[1152,1536]{1,0:T(8,128)(2,1)} %bitcast.2, f32[1,1536]{1,0:T(1,128)} %cb_hbm.1, bf16[1536,1024]{1,0:T(8,128)(2,1)} %hw_hbm.1, f32[1,1024]{1,0:T(1,128)} %bitcast.3), custom_call_target="tpu_custom_call" | custom-call | tf_op jit(solution)/shard_map/pallas_call | solution.py:392
  53.0 2.5 %multiply_convert_fusion = bf16[384,1024]{1,0:T(8,128)(2,1)} fusion(bf16[384,1024]{1,0:T(8,128)(2,1)} %get-tuple-element.8, bf16[384,1024]{1,0:T(8,128)(2,1)} %get-tuple-element.7), kind=kLoop, calls=%fused_computation | loop fusion | flops 1966080 | bytes 2359296 | tf_op jit(solution)/shard_map/convert_element_type | solution.py:424
